TPU v7x, 512 devices: a whole 4x4x16 slice. The times are simulated.
512 devices in a mesh: dom: 512 (over z, y, x, core).
Axes of the slice: x: 4, y: 4, z: 16, core: 2. Of those that a mesh axis runs over, the one named last changes fastest.
Arguments:
- features: bfloat16 [131072, 256], P('dom'), may hold values from -48 to 48
- w_query: bfloat16 [256, 256], replicated, may hold values from -0.375 to 0.375
- w_key: bfloat16 [256, 256], replicated, may hold values from -0.375 to 0.375
- w_value: bfloat16 [256, 256], replicated, may hold values from -0.375 to 0.375
- w_out: bfloat16 [256, 256], replicated, may hold values from -0.375 to 0.375
- local_blocks: int32 [1024, 4], P('dom'), may hold values from 0 to 3, as said below
- local_count: int32 [1024], P('dom'), may hold values from 1 to 4, as said below
- expander_blocks: int32 [4, 1024, 2], P(None, 'dom'), may hold values from 0 to 1, as said below
- expander_count: int32 [4, 1024], P(None, 'dom'), may hold values from 1 to 2, as said below
Outputs:
- updated: bfloat16 [131072, 256], P('dom')
Inputs may be any that keep to these rules, and one draw needn't show every extreme that they name: `local_blocks`: each row names 4 different positions of the extended range; the row of each partition's first block begins with position 0 and that of its last block with position 3. `local_count`: loads differ from partition to partition; block 0 of every partition uses its partition's largest count. `expander_blocks`: each row names 2 different blocks. `expander_count`: loads differ from partition to partition; block 0 of every partition uses its partition's largest count.
All inputs are finite; a program needn't handle non-finite values.
Results may differ from a plain program's by a relative error of at most 0.0065.
Values may be sent and summed in bfloat16 or wider, within the bound.
A program may use at most 64 MiB of HBM per device.

v0:
```python
import jax
import jax.numpy as jnp
from jax import lax
from jax.sharding import PartitionSpec as P

HEADS = 8


epsilon = 1e-06


def extended_2(array, sides, width):
    for axis, dim in sides:
        peers, length = (lax.axis_size(axis), array.shape[dim])
        up = [(i, (i + 1) % peers) for i in range(peers)]
        down = [(j, i) for i, j in up]
        last = lax.slice_in_dim(array, length - width, length, axis=dim)
        leading = lax.slice_in_dim(array, 0, width, axis=dim)
        before = lax.ppermute(last, axis, up)
        after = lax.ppermute(leading, axis, down)
        array = jnp.concatenate([before, array, after], axis=dim)
    return array


def partner_2(block, axis, apart):
    count = lax.axis_size(axis)
    route = []
    for low in range(count):
        high = low | 1 << apart
        if high != low and high < count:
            route += [(low, high), (high, low)]
    return lax.ppermute(block, axis, route)


def part_state(queries, kv_blocks, chosen, live_count):
    picked = kv_blocks[chosen]
    slot_count = chosen.shape[0]
    block_rows = kv_blocks.shape[1]
    head_size = queries.shape[-1]
    picked = picked.reshape(slot_count * block_rows, 2, HEADS, head_size)
    key_rows = picked[:, 0]
    values = picked[:, 1]
    scores = jnp.einsum("qhd,khd->hqk", queries, key_rows, preferred_element_type=jnp.float32)
    usable = jnp.arange(slot_count * block_rows, dtype=jnp.int32) // block_rows < live_count
    scores = jnp.where(usable[None, None, :], scores, jnp.float32(-1e30))
    row_max = jnp.max(scores, axis=-1)
    weights = jnp.where(
        usable[None, None, :], jnp.exp(scores - row_max[..., None]), jnp.float32(0.0)
    )
    weights = weights.astype(jnp.bfloat16)
    weight_sum = jnp.sum(weights.astype(jnp.float32), axis=-1)
    context = jnp.einsum("hqk,khd->hqd", weights, values, preferred_element_type=jnp.float32)
    return (row_max, weight_sum, context)


def block_states(queries, kv_blocks, chosen, live_count):
    return jax.vmap(part_state, in_axes=(0, None, 0, 0))(queries, kv_blocks, chosen, live_count)


def combine(states):
    tops = jnp.stack([s[0] for s in states])
    sums = jnp.stack([s[1] for s in states])
    outs = jnp.stack([s[2] for s in states])
    highest = jnp.max(tops, axis=0)
    factor = jnp.exp(tops - highest[None])
    total = jnp.sum(factor * sums, axis=0)
    merged = jnp.sum(factor[..., None] * outs, axis=0)
    return merged / total[..., None]


def shards(
    features,
    w_query,
    w_key,
    w_value,
    w_out,
    local_blocks,
    local_count,
    expander_blocks,
    expander_count,
):
    row_count, feature_width = features.shape
    group_count = local_blocks.shape[0]
    block_rows = row_count // group_count
    head_size = feature_width // HEADS
    scaling = float(head_size) ** (-0.5)
    queries = (jnp.dot(features, w_query, preferred_element_type=jnp.float32) * scaling).astype(
        jnp.bfloat16
    )
    queries = queries.reshape(group_count, block_rows, HEADS, head_size)
    w_pair = jnp.concatenate([w_key, w_value], axis=1)
    pairs = jnp.dot(features, w_pair, preferred_element_type=jnp.float32).astype(jnp.bfloat16)
    padded = extended_2(pairs, (("dom", 0),), block_rows)
    extended = padded.reshape(group_count + 2, block_rows, 2 * feature_width)
    states = [block_states(queries, extended, local_blocks, local_count)]
    levels = lax.axis_size("dom").bit_length() - 1
    match_total = expander_blocks.shape[0]
    for matching in range(match_total):
        swap_bit = matching * levels // match_total
        partner = partner_2(pairs, "dom", swap_bit)
        partner_blocks = partner.reshape(group_count, block_rows, 2 * feature_width)
        states.append(
            block_states(
                queries, partner_blocks, expander_blocks[matching], expander_count[matching]
            )
        )
    merged = combine(states)
    context = (
        jnp.transpose(merged, (0, 2, 1, 3)).reshape(row_count, feature_width).astype(jnp.bfloat16)
    )
    mixed = jnp.dot(context, w_out, preferred_element_type=jnp.float32)
    normed = mixed / jnp.sqrt(jnp.mean(mixed * mixed, axis=-1, keepdims=True) + epsilon)
    return (features.astype(jnp.float32) + normed).astype(jnp.bfloat16)


def solution(mesh):
    in_specs = (
        P("dom", None),
        P(),
        P(),
        P(),
        P(),
        P("dom", None),
        P("dom"),
        P(None, "dom", None),
        P(None, "dom"),
    )
    out_specs = P("dom", None)
    return jax.shard_map(shards, mesh=mesh, in_specs=in_specs, out_specs=out_specs, check_vma=False)
```

profile of v0, /device:TPU:64, one launch (start us, length us, event | category | flops | bytes accessed | tf_op | source)
XLA Modules:
  0.0 72.4 jit_solution(12246336924060730686)
XLA Ops:
  0.0 2.0 %fusion = bf16[256,512]{1,0:T(8,128)(2,1)} fusion(bf16[256,256]{1,0:T(8,128)(2,1)} %param.9, bf16[256,256]{1,0:T(8,128)(2,1)} %param.12, bf16[256,256]{1,0:T(8,128)(2,1)} %param.11), kind=kOutput, calls=%fused_computation.22 | convolution fusion | flops 67764224 | bytes 655360 | tf_op jit(solution)/shard_map/dot_general | solution.py:92
  2.0 1.9 %collective-permute-start.2 = (bf16[256,512]{1,0:T(8,128)(2,1)}, bf16[256,512]{1,0:T(8,128)(2,1)}, u32[]{:S(2)}, u32[]{:S(2)}) collective-permute-start(bf16[256,512]{1,0:T(8,128)(2,1)} %fusion), channel_id=1, source_target_pairs={{0,1},{1,0},{2,3},{3,2},{4,5},{5,4},{6,7},{7,6},{8,9},{9,8},{10,11... | collective-permute-start | bytes 786440 | tf_op jit(solution)/shard_map/ppermute | solution.py:32
  3.9 4.9 %collective-permute-start.3 = (bf16[256,512]{1,0:T(8,128)(2,1)}, bf16[256,512]{1,0:T(8,128)(2,1)}, u32[]{:S(2)}, u32[]{:S(2)}) collective-permute-start(bf16[256,512]{1,0:T(8,128)(2,1)} %fusion), channel_id=1, source_target_pairs={{0,4},{4,0},{1,5},{5,1},{2,6},{6,2},{3,7},{7,3},{8,12},{12,8},{9,1... | collective-permute-start | bytes 786440 | tf_op jit(solution)/shard_map/ppermute | solution.py:32
  8.8 5.1 %collective-permute-start.4 = (bf16[256,512]{1,0:T(8,128)(2,1)}, bf16[256,512]{1,0:T(8,128)(2,1)}, u32[]{:S(2)}, u32[]{:S(2)}) collective-permute-start(bf16[256,512]{1,0:T(8,128)(2,1)} %fusion), channel_id=1, source_target_pairs={{0,16},{16,0},{1,17},{17,1},{2,18},{18,2},{3,19},{19,3},{4,20},{20... | collective-permute-start | bytes 786440 | tf_op jit(solution)/shard_map/ppermute | solution.py:32
  14.0 1.0 %fusion.43 = (bf16[128,512]{1,0:T(8,128)(2,1)S(1)}, bf16[128,512]{1,0:T(8,128)(2,1)S(1)}) fusion(bf16[256,512]{1,0:T(8,128)(2,1)} %fusion), kind=kLoop, calls=%fused_computation.130 | loop fusion | bytes 524288 | tf_op jit(solution)/shard_map/slice | solution.py:17
  15.0 2.6 %collective-permute-start.1 = (bf16[128,512]{1,0:T(8,128)(2,1)S(1)}, bf16[128,512]{1,0:T(8,128)(2,1)S(1)}, u32[]{:S(2)}, u32[]{:S(2)}) collective-permute-start(bf16[128,512]{1,0:T(8,128)(2,1)S(1)} %get-tuple-element.26), channel_id=1, source_target_pairs={{1,0},{2,1},{3,2},{4,3},{5,4},{6,5},{7,6},{8,7},{9,8},{10,9},{11,1... | collective-permute-start | bytes 393224 | tf_op jit(solution)/shard_map/ppermute | solution.py:20
  17.6 1.9 %collective-permute-start = (bf16[128,512]{1,0:T(8,128)(2,1)S(1)}, bf16[128,512]{1,0:T(8,128)(2,1)S(1)}, u32[]{:S(2)}, u32[]{:S(2)}) collective-permute-start(bf16[128,512]{1,0:T(8,128)(2,1)S(1)} %get-tuple-element.25), channel_id=1, source_target_pairs={{0,1},{1,2},{2,3},{3,4},{4,5},{5,6},{6,7},{7,8},{8,9},{9,10},{10,1... | collective-permute-start | bytes 393224 | tf_op jit(solution)/shard_map/ppermute | solution.py:19
  19.5 0.7 compare_select_fusion.4
  20.3 1.2 %fusion.6 = bf16[256,256]{1,0:T(8,128)(2,1)S(1)} fusion(bf16[256,256]{1,0:T(8,128)(2,1)} %param.9, bf16[256,256]{1,0:T(8,128)(2,1)} %param.10), kind=kOutput, calls=%fused_computation.34 | convolution fusion | flops 33685504 | bytes 393216 | tf_op jit(solution)/shard_map/dot_general | solution.py:87
  21.5 1.1 %slice_reduce_fusion = (s32[2,2]{1,0:T(2,128)S(1)}, s32[2,2]{1,0:T(2,128)S(1)}, s32[2,2]{1,0:T(2,128)S(1)}, s32[2,2]{1,0:T(2,128)S(1)}) fusion(s32[4,2,2]{0,2,1:T(2,128)} %param.16), kind=kLoop, calls=%fused_computation.95 | loop fusion | bytes 128 | tf_op jit(solution)/shard_map/slice | solution.py:104
  22.7 0.6 pad_clamp_fusion.3
  23.3 1.0 %slice_reduce_fusion.4 = (s32[2]{0:T(128)S(1)}, s32[2]{0:T(128)S(1)}, s32[2]{0:T(128)S(1)}, s32[2]{0:T(128)S(1)}) fusion(s32[4,2]{0,1:T(2,128)} %param.17), kind=kLoop, calls=%fused_computation.106 | loop fusion | bytes 64 | tf_op jit(solution)/shard_map/slice | solution.py:104
  24.4 0.6 pad_clamp_fusion.2
  25.1 0.7 %broadcast_compare_fusion = pred[2,512]{1,0:T(4,128)(4,1)S(1)} fusion(s32[512]{0:T(512)S(1)} %add_select_fusion, s32[2]{0:T(128)} %param.15), kind=kLoop, calls=%fused_computation.102 | loop fusion | flops 1024 | bytes 3080 | tf_op jit(solution)/shard_map/vmap()/lt | solution.py:44
  25.8 0.7 broadcast_compare_fusion.1
  26.5 0.6 pad_clamp_fusion.1
  27.1 1.0 %copy.58 = bf16[256,256]{0,1:T(8,128)(2,1)S(1)} copy(bf16[256,256]{1,0:T(8,128)(2,1)} %param.9) | data formatting | bytes 262144 | tf_op args[0]
  28.1 0.1 copy.59
  28.3 0.6 pad_clamp_fusion
  28.9 10.9 %collective-permute-start.5 = (bf16[256,512]{1,0:T(8,128)(2,1)}, bf16[256,512]{1,0:T(8,128)(2,1)}, u32[]{:S(2)}, u32[]{:S(2)}) collective-permute-start(bf16[256,512]{1,0:T(8,128)(2,1)} %fusion), channel_id=1, source_target_pairs={{0,64},{64,0},{1,65},{65,1},{2,66},{66,2},{3,67},{67,3},{4,68},{68... | collective-permute-start | bytes 786440 | tf_op jit(solution)/shard_map/ppermute | solution.py:32
  39.9 1.0 %pad_maximum_fusion = bf16[512,512]{1,0:T(8,128)(2,1)S(1)} fusion(bf16[128,512]{1,0:T(8,128)(2,1)S(1)} %collective-permute-done.1, bf16[256,512]{1,0:T(8,128)(2,1)} %fusion, bf16[128,512]{1,0:T(8,128)(2,1)S(1)} %collective-permute-done), kind=kLoop, calls=%fused_computation.35 | loop fusion | flops 1572864 | bytes 1048576 | tf_op jit(solution)/shard_map/concatenate | solution.py:21
  40.9 0.6 gather_fusion
  41.5 0.8 %copy.60 = bf16[8,128,512]{1,0,2:T(8,128)(2,1)S(1)} copy(bf16[8,128,512]{2,1,0:T(8,128)(2,1)S(1)} %gather_fusion) | data formatting | bytes 2097152 | tf_op jit(solution)/shard_map/vmap()/gather | solution.py:36
  42.3 0.4 reshape.382
  42.7 0.7 fusion.38
  43.4 0.8 %select_reduce_fusion = (f32[2,8,128]{2,1,0:T(8,128)S(1)}, f32[2,8,128,512]{3,2,1,0:T(8,128)S(1)}) fusion(pred[2,512]{1,0:T(4,128)(4,1)S(1)} %broadcast_compare_fusion, bf16[2,512,1,8,32]{1,0,4,3,2:T(2,128)(2,1)S(1)} %get-tuple-element.15, bf16[2,128,8,32]{1,0,3,2:T(2,128)(2,1)S(1)} %reshape.380), kind=kOutput, calls=%fused_computation.7 | convolution fusion | flops 69203968 | bytes 4858880 | tf_op jit(solution)/shard_map/vmap(qhd,khd->hqk)/dot_general | solution.py:43
  44.3 1.2 %convert_reduce_fusion = f32[2,8,128]{2,1,0:T(8,128)S(1)} fusion(f32[2,8,128]{2,1,0:T(8,128)S(1)} %get-tuple-element.31, f32[2,8,128,512]{3,2,1,0:T(8,128)S(1)} %get-tuple-element.32, pred[2,512]{1,0:T(4,128)(4,1)S(1)} %broadcast_compare_fusion), kind=kLoop, calls=%fused_computation.5 | loop fusion | flops 6289408 | bytes 4211712 | tf_op jit(solution)/shard_map/vmap()/reduce_sum | solution.py:51
  45.4 1.3 %fusion.1 = f32[5,2,8,128,32]{3,4,2,1,0:T(8,128)S(1)} fusion(bf16[2,512,1,8,32]{1,0,4,3,2:T(2,128)(2,1)S(1)} %get-tuple-element.16, f32[2,8,128,512]{3,2,1,0:T(8,128)S(1)} %get-tuple-element.32, f32[2,8,128]{2,1,0:T(8,128)S(1)} %get-tuple-element.31, pred[2,512]{1,0:T(4,128)(4,1)S(1)} %broadcast_compare_fusion), kind=kOutput, calls=%fused_computation.24 | convolution fusion | flops 71303168 | bytes 4989952 | tf_op jit(solution)/shard_map/vmap(hqk,khd->hqd)/dot_general | solution.py:52
  46.7 0.6 constant_dynamic-update-slice_fusion.4
  47.3 0.6 constant_dynamic-update-slice_fusion.9
  47.9 1.7 %gather_fusion.1 = bf16[4,128,512]{2,1,0:T(8,128)(2,1)S(1)} fusion(bf16[2,128,512]{2,1,0:T(8,128)(2,1)} %bitcast.4, s32[1024]{0:T(1024)} %pad_clamp_fusion.3), kind=kCustom, calls=%fused_computation.1 | custom fusion | bytes 1048592 | tf_op jit(solution)/shard_map/vmap()/gather | solution.py:36
  49.6 0.3 copy.63
  49.9 0.3 reshape.384
  50.2 1.2 %fusion.42 = (bf16[2,256,1,8,32]{1,0,4,3,2:T(2,128)(2,1)S(1)}, bf16[2,256,1,8,32]{1,0,4,3,2:T(2,128)(2,1)}) fusion(bf16[2,256,2,8,32]{1,0,4,3,2:T(2,128)(2,1)S(1)} %reshape.384), kind=kLoop, calls=%fused_computation.129 | loop fusion | bytes 1048576 | tf_op jit(solution)/shard_map/vmap()/slice | solution.py:41
  51.4 1.7 %gather_fusion.2 = bf16[4,128,512]{2,1,0:T(8,128)(2,1)S(1)} fusion(bf16[2,128,512]{2,1,0:T(8,128)(2,1)} %bitcast.7, s32[1024]{0:T(1024)} %pad_clamp_fusion.2), kind=kCustom, calls=%fused_computation.2 | custom fusion | bytes 1048592 | tf_op jit(solution)/shard_map/vmap()/gather | solution.py:36
  53.1 0.3 copy.66
  53.4 0.3 reshape.386
  53.7 1.2 %fusion.41 = (bf16[2,256,1,8,32]{1,0,4,3,2:T(2,128)(2,1)S(1)}, bf16[2,256,1,8,32]{1,0,4,3,2:T(2,128)(2,1)}) fusion(bf16[2,256,2,8,32]{1,0,4,3,2:T(2,128)(2,1)S(1)} %reshape.386), kind=kLoop, calls=%fused_computation.128 | loop fusion | bytes 1048576 | tf_op jit(solution)/shard_map/vmap()/slice | solution.py:41
  54.9 1.7 %gather_fusion.3 = bf16[4,128,512]{2,1,0:T(8,128)(2,1)S(1)} fusion(bf16[2,128,512]{2,1,0:T(8,128)(2,1)} %bitcast.10, s32[1024]{0:T(1024)} %pad_clamp_fusion.1), kind=kCustom, calls=%fused_computation.3 | custom fusion | bytes 1048592 | tf_op jit(solution)/shard_map/vmap()/gather | solution.py:36
  56.6 0.3 copy.69
  56.9 0.3 reshape.388
  57.2 1.2 %fusion.40 = (bf16[2,256,1,8,32]{1,0,4,3,2:T(2,128)(2,1)S(1)}, bf16[2,256,1,8,32]{1,0,4,3,2:T(2,128)(2,1)}) fusion(bf16[2,256,2,8,32]{1,0,4,3,2:T(2,128)(2,1)S(1)} %reshape.388), kind=kLoop, calls=%fused_computation.127 | loop fusion | bytes 1048576 | tf_op jit(solution)/shard_map/vmap()/slice | solution.py:41
  58.4 1.7 %gather_fusion.4 = bf16[4,128,512]{2,1,0:T(8,128)(2,1)S(1)} fusion(bf16[2,128,512]{2,1,0:T(8,128)(2,1)} %bitcast.13, s32[1024]{0:T(1024)} %pad_clamp_fusion), kind=kCustom, calls=%fused_computation.4 | custom fusion | bytes 1048592 | tf_op jit(solution)/shard_map/vmap()/gather | solution.py:36
  60.1 0.3 copy.72
  60.4 0.3 reshape.390
  60.7 0.4 fusion.39
  61.1 1.2 %select_reduce_fusion.4 = (f32[2,8,128]{2,1,0:T(8,128)S(1)}, f32[2,8,128,256]{3,2,1,0:T(8,128)S(1)}) fusion(pred[2,256]{1,0:T(4,128)(4,1)} %get-tuple-element.30, bf16[2,256,1,8,32]{1,0,4,3,2:T(2,128)(2,1)S(1)} %get-tuple-element.23, bf16[2,128,8,32]{1,0,3,2:T(2,128)(2,1)S(1)} %reshape.380), kind=kOutput, calls=%fused_computation.19 | convolution fusion | flops 34600960 | bytes 2499072 | tf_op jit(solution)/shard_map/vmap(qhd,khd->hqk)/dot_general | solution.py:43
  62.4 0.6 select_reduce_fusion.3
  63.0 0.6 select_reduce_fusion.2
  63.5 0.6 select_reduce_fusion.1
  64.1 0.8 %convert_reduce_fusion.4 = f32[2,8,128]{2,1,0:T(8,128)S(1)} fusion(f32[2,8,128]{2,1,0:T(8,128)S(1)} %get-tuple-element.33, f32[2,8,128,256]{3,2,1,0:T(8,128)S(1)} %get-tuple-element.34, pred[2,256]{1,0:T(4,128)(4,1)S(1)} %copy-done.8), kind=kLoop, calls=%fused_computation.11 | loop fusion | flops 3143680 | bytes 2114048 | tf_op jit(solution)/shard_map/vmap()/reduce_sum | solution.py:51
  65.0 0.8 %convert_reduce_fusion.3 = f32[2,8,128]{2,1,0:T(8,128)S(1)} fusion(f32[2,8,128]{2,1,0:T(8,128)S(1)} %get-tuple-element.35, f32[2,8,128,256]{3,2,1,0:T(8,128)S(1)} %get-tuple-element.36, pred[2,256]{1,0:T(4,128)(4,1)S(1)} %copy-done.7), kind=kLoop, calls=%fused_computation.10 | loop fusion | flops 3143680 | bytes 2114048 | tf_op jit(solution)/shard_map/vmap()/reduce_sum | solution.py:51
  65.8 0.8 %convert_reduce_fusion.2 = f32[2,8,128]{2,1,0:T(8,128)S(1)} fusion(f32[2,8,128]{2,1,0:T(8,128)S(1)} %get-tuple-element.37, f32[2,8,128,256]{3,2,1,0:T(8,128)S(1)} %get-tuple-element.38, pred[2,256]{1,0:T(4,128)(4,1)S(1)} %copy-done.6), kind=kLoop, calls=%fused_computation.9 | loop fusion | flops 3143680 | bytes 2114048 | tf_op jit(solution)/shard_map/vmap()/reduce_sum | solution.py:51
  66.7 0.8 %convert_reduce_fusion.1 = f32[2,8,128]{2,1,0:T(8,128)S(1)} fusion(f32[2,8,128]{2,1,0:T(8,128)S(1)} %get-tuple-element.39, f32[2,8,128,256]{3,2,1,0:T(8,128)S(1)} %get-tuple-element.40, pred[2,256]{1,0:T(4,128)(4,1)S(1)} %get-tuple-element.27), kind=kLoop, calls=%fused_computation.8 | loop fusion | flops 3143680 | bytes 2114048 | tf_op jit(solution)/shard_map/vmap()/reduce_sum | solution.py:51
  67.6 0.8 %fusion.5 = f32[5,2,8,128,32]{3,4,2,1,0:T(8,128)S(1)} fusion(f32[5,2,8,128,32]{3,4,2,1,0:T(8,128)S(1)} %fusion.1, bf16[2,256,1,8,32]{1,0,4,3,2:T(2,128)(2,1)S(1)} %copy-done.1, f32[2,8,128,256]{3,2,1,0:T(8,128)S(1)} %get-tuple-element.34, f32[2,8,128]{2,1,0:T(8,128)S(1)} %get-tuple-element.33, pred[2,256]{1,0:T(4,128)(4,1)S(1)} %copy-done.8), kind=kOutput, calls=%fused_computation.33 | convolution fusion | flops 35651584 | bytes 2630656 | tf_op jit(solution)/shard_map/vmap(hqk,khd->hqd)/dot_general | solution.py:52
  68.4 0.1 copy-done.2
  68.5 0.8 %fusion.4 = f32[5,2,8,128,32]{3,4,2,1,0:T(8,128)S(1)} fusion(f32[5,2,8,128,32]{3,4,2,1,0:T(8,128)S(1)} %fusion.5, bf16[2,256,1,8,32]{1,0,4,3,2:T(2,128)(2,1)S(1)} %copy-done.2, f32[2,8,128,256]{3,2,1,0:T(8,128)S(1)} %get-tuple-element.36, f32[2,8,128]{2,1,0:T(8,128)S(1)} %get-tuple-element.35, pred[2,256]{1,0:T(4,128)(4,1)S(1)} %copy-done.7), kind=kOutput, calls=%fused_computation.31 | convolution fusion | flops 35651584 | bytes 2630656 | tf_op jit(solution)/shard_map/vmap(hqk,khd->hqd)/dot_general | solution.py:52
  69.2 0.1 copy-done.3
  69.3 0.8 %fusion.3 = f32[5,2,8,128,32]{3,4,2,1,0:T(8,128)S(1)} fusion(f32[5,2,8,128,32]{3,4,2,1,0:T(8,128)S(1)} %fusion.4, bf16[2,256,1,8,32]{1,0,4,3,2:T(2,128)(2,1)S(1)} %copy-done.3, f32[2,8,128,256]{3,2,1,0:T(8,128)S(1)} %get-tuple-element.38, f32[2,8,128]{2,1,0:T(8,128)S(1)} %get-tuple-element.37, pred[2,256]{1,0:T(4,128)(4,1)S(1)} %copy-done.6), kind=kOutput, calls=%fused_computation.29 | convolution fusion | flops 35651584 | bytes 2630656 | tf_op jit(solution)/shard_map/vmap(hqk,khd->hqd)/dot_general | solution.py:52
  70.1 0.8 %fusion.2 = f32[5,2,8,128,32]{3,4,2,1,0:T(8,128)S(1)} fusion(f32[5,2,8,128,32]{3,4,2,1,0:T(8,128)S(1)} %fusion.3, bf16[2,256,1,8,32]{1,0,4,3,2:T(2,128)(2,1)S(1)} %get-tuple-element.18, f32[2,8,128,256]{3,2,1,0:T(8,128)S(1)} %get-tuple-element.40, f32[2,8,128]{2,1,0:T(8,128)S(1)} %get-tuple-element.39, pred[2,256]{1,0:T(4,128)(4,1)S(1)} %get-tuple-element.27), kind=kOutput, calls=%fused_computation.27 | convolution fusion | flops 35651584 | bytes 2630656 | tf_op jit(solution)/shard_map/vmap(hqk,khd->hqd)/dot_general | solution.py:52
  70.9 0.2 multiply_reduce_fusion
  71.2 0.1 copy.80
  71.3 0.3 multiply_reduce_fusion.1
  71.6 0.8 %copy.81 = bf16[256,256]{1,0:T(8,128)(2,1)} copy(bf16[256,256]{0,1:T(8,128)(2,1)S(1)} %add_convert_fusion) | data formatting | bytes 262144 | tf_op jit(solution)/shard_map/convert_element_type | solution.py:113
  (46 shorter events, 0.7 us)
Async XLA Ops:
  0.0 71.3 %copy-start = (bf16[256,256]{1,0:T(8,128)(2,1)S(1)}, bf16[256,256]{1,0:T(8,128)(2,1)}, u32[]{:S(2)}) copy-start(bf16[256,256]{1,0:T(8,128)(2,1)} %param.13) | copy-start | bytes 393220
  2.0 45.9 %collective-permute-start.2 = (bf16[256,512]{1,0:T(8,128)(2,1)}, bf16[256,512]{1,0:T(8,128)(2,1)}, u32[]{:S(2)}, u32[]{:S(2)}) collective-permute-start(bf16[256,512]{1,0:T(8,128)(2,1)} %fusion), channel_id=1, source_target_pairs={{0,1},{1,0},{2,3},{3,2},{4,5},{5,4},{6,7},{7,6},{8,9},{9,8},{10,11... | collective-permute-start | bytes 786440 | tf_op jit(solution)/shard_map/ppermute | solution.py:32
  3.9 47.5 %collective-permute-start.3 = (bf16[256,512]{1,0:T(8,128)(2,1)}, bf16[256,512]{1,0:T(8,128)(2,1)}, u32[]{:S(2)}, u32[]{:S(2)}) collective-permute-start(bf16[256,512]{1,0:T(8,128)(2,1)} %fusion), channel_id=1, source_target_pairs={{0,4},{4,0},{1,5},{5,1},{2,6},{6,2},{3,7},{7,3},{8,12},{12,8},{9,1... | collective-permute-start | bytes 786440 | tf_op jit(solution)/shard_map/ppermute | solution.py:32
  8.8 46.1 %collective-permute-start.4 = (bf16[256,512]{1,0:T(8,128)(2,1)}, bf16[256,512]{1,0:T(8,128)(2,1)}, u32[]{:S(2)}, u32[]{:S(2)}) collective-permute-start(bf16[256,512]{1,0:T(8,128)(2,1)} %fusion), channel_id=1, source_target_pairs={{0,16},{16,0},{1,17},{17,1},{2,18},{18,2},{3,19},{19,3},{4,20},{20... | collective-permute-start | bytes 786440 | tf_op jit(solution)/shard_map/ppermute | solution.py:32
  15.0 14.0 %collective-permute-start.1 = (bf16[128,512]{1,0:T(8,128)(2,1)S(1)}, bf16[128,512]{1,0:T(8,128)(2,1)S(1)}, u32[]{:S(2)}, u32[]{:S(2)}) collective-permute-start(bf16[128,512]{1,0:T(8,128)(2,1)S(1)} %get-tuple-element.26), channel_id=1, source_target_pairs={{1,0},{2,1},{3,2},{4,3},{5,4},{6,5},{7,6},{8,7},{9,8},{10,9},{11,1... | collective-permute-start | bytes 393224 | tf_op jit(solution)/shard_map/ppermute | solution.py:20
  17.6 22.3 %collective-permute-start = (bf16[128,512]{1,0:T(8,128)(2,1)S(1)}, bf16[128,512]{1,0:T(8,128)(2,1)S(1)}, u32[]{:S(2)}, u32[]{:S(2)}) collective-permute-start(bf16[128,512]{1,0:T(8,128)(2,1)S(1)} %get-tuple-element.25), channel_id=1, source_target_pairs={{0,1},{1,2},{2,3},{3,4},{4,5},{5,6},{6,7},{7,8},{8,9},{9,10},{10,1... | collective-permute-start | bytes 393224 | tf_op jit(solution)/shard_map/ppermute | solution.py:19
  28.9 29.5 %collective-permute-start.5 = (bf16[256,512]{1,0:T(8,128)(2,1)}, bf16[256,512]{1,0:T(8,128)(2,1)}, u32[]{:S(2)}, u32[]{:S(2)}) collective-permute-start(bf16[256,512]{1,0:T(8,128)(2,1)} %fusion), channel_id=1, source_target_pairs={{0,64},{64,0},{1,65},{65,1},{2,66},{66,2},{3,67},{67,3},{4,68},{68... | collective-permute-start | bytes 786440 | tf_op jit(solution)/shard_map/ppermute | solution.py:32
  60.7 1.7 %copy-start.7 = (pred[2,256]{1,0:T(4,128)(4,1)S(1)}, pred[2,256]{1,0:T(4,128)(4,1)}, u32[]{:S(2)}) copy-start(pred[2,256]{1,0:T(4,128)(4,1)} %get-tuple-element.28) | copy-start | bytes 1540
  61.1 1.8 %copy-start.6 = (pred[2,256]{1,0:T(4,128)(4,1)S(1)}, pred[2,256]{1,0:T(4,128)(4,1)}, u32[]{:S(2)}) copy-start(pred[2,256]{1,0:T(4,128)(4,1)} %get-tuple-element.29) | copy-start | bytes 1540
  63.0 1.1 %copy-start.8 = (pred[2,256]{1,0:T(4,128)(4,1)S(1)}, pred[2,256]{1,0:T(4,128)(4,1)}, u32[]{:S(2)}) copy-start(pred[2,256]{1,0:T(4,128)(4,1)} %get-tuple-element.30) | copy-start | bytes 1540
  65.8 1.7 %copy-start.5 = (f32[5,2,8,128]{3,2,1,0:T(8,128)S(1)}, f32[5,2,8,128]{3,2,1,0:T(8,128)}, u32[]{:S(2)}) copy-start(f32[5,2,8,128]{3,2,1,0:T(8,128)} %constant_dynamic-update-slice_fusion.4) | copy-start | bytes 122884
  65.8 1.8 %copy-start.1 = (bf16[2,256,1,8,32]{1,0,4,3,2:T(2,128)(2,1)S(1)}, bf16[2,256,1,8,32]{1,0,4,3,2:T(2,128)(2,1)}, u32[]{:S(2)}) copy-start(bf16[2,256,1,8,32]{1,0,4,3,2:T(2,128)(2,1)} %get-tuple-element.24) | copy-start | bytes 786436
  67.5 1.0 %copy-start.2 = (bf16[2,256,1,8,32]{1,0,4,3,2:T(2,128)(2,1)S(1)}, bf16[2,256,1,8,32]{1,0,4,3,2:T(2,128)(2,1)}, u32[]{:S(2)}) copy-start(bf16[2,256,1,8,32]{1,0,4,3,2:T(2,128)(2,1)} %get-tuple-element.22) | copy-start | bytes 786436
  68.4 1.0 %copy-start.3 = (bf16[2,256,1,8,32]{1,0,4,3,2:T(2,128)(2,1)S(1)}, bf16[2,256,1,8,32]{1,0,4,3,2:T(2,128)(2,1)}, u32[]{:S(2)}) copy-start(bf16[2,256,1,8,32]{1,0,4,3,2:T(2,128)(2,1)} %get-tuple-element.20) | copy-start | bytes 786436
  70.1 0.8 %copy-start.4 = (f32[5,2,8,128]{3,2,1,0:T(8,128)S(1)}, f32[5,2,8,128]{3,2,1,0:T(8,128)}, u32[]{:S(2)}) copy-start(f32[5,2,8,128]{3,2,1,0:T(8,128)} %constant_dynamic-update-slice_fusion.9) | copy-start | bytes 122884
where the time goes:
time: 73.1 us; the launch traced here: 72.4 us
  starting transfers between devices  27.4 us (37%)
  local copies, waits for them, and re-layouts  22.7 us (31%)
  matrix products  11.5 us (16%)
  other arithmetic  10.3 us (14%)
    ppermute x4, starting transfers between devices, partner_2(): return lax.ppermute(block, axis, route)  22.9 us
    gather x10, local copies, waits for them, and re-layouts, part_state(): picked = kv_blocks[chosen]  9.22 us
    slice x5, local copies, waits for them, and re-layouts, part_state(): key_rows = picked[:, 0]  4.65 us
    reduce_sum x5, other arithmetic, part_state(): weight_sum = jnp.sum(weights.astype(jnp.float32), axis=-1)  4.5 us
    dot_general x5, matrix products, part_state(): jnp.einsum('hqk,khd->hqd', weights, values, preferred_element_type=jnp.fl...  4.3 us
    dot_general x5, matrix products, part_state(): jnp.einsum('qhd,khd->hqk', queries, key_rows, preferred_element_type=jnp....  3.77 us
    ppermute x1, starting transfers between devices, extended_2(): after = lax.ppermute(leading, axis, down)  2.62 us
    unnamed x27, local copies, waits for them, and re-layouts  2.49 us
  transfers between devices with their start and end apart: 6, of which 0 were waited for; matrix products, arithmetic and copies ran while one was open for 40% of the time, Pallas kernels for 0%

commit v1 on v0

v1 whole, which is shorter than its diff:
```python
import functools

import jax
import jax.numpy as jnp
from jax import lax
from jax.experimental import pallas as pl
from jax.experimental.pallas import tpu as pltpu
from jax.sharding import PartitionSpec as P

HEADS = 8
BLK = 128
EPS = 1e-06
LOG2E = 1.4426950408889634
OFF = -1e30
FLOOR = -1e20
MESH = pl.DeviceIdType.MESH
F32 = jnp.float32
BF16 = jnp.bfloat16
CORE, XX, YY, HALO, ZZ = range(5)


def flip(me, apart):
    wide = 1 << apart
    return me + wide - 2 * wide * ((me // wide) % 2)


def dot(a, b, over):
    return lax.dot_general(a, b, ((over[0], over[1]), ((), ())), preferred_element_type=F32)


def attend_kernel(
    peers, swaps,
    f_hbm, wq_hbm, wk_hbm, wv_hbm, lb_hbm, lc_hbm, eb_hbm, ec_hbm,
    ctx_ref,
    own, wq, wk, wv, lb, lc, eb, ec,
    kv, g, wvt, vt, bias, top, acc,
    local_sem, send_sem, recv_sem, ready_sem,
):
    me = lax.axis_index("dom")
    odd = me % 2
    rows = own.shape[0]
    width = own.shape[1]
    head = width // HEADS
    beside = lax.rem(me + 2 * odd - 1 + peers, peers)
    partner = [flip(me, swaps[0]), flip(me, swaps[1]), flip(me, swaps[2]), beside, flip(me, swaps[3])]

    def waits(apart):
        low = 1 << apart
        usual = (me // low) % 2
        return jnp.where(me == 0, 1, jnp.where(me == low, 0, usual))

    even_end = me + odd
    late = [
        1 - odd,
        waits(swaps[1]),
        waits(swaps[2]),
        jnp.where(even_end % 8 == 0, odd, 1 - odd),
        waits(swaps[3]),
    ]

    barrier = pltpu.get_barrier_semaphore()
    for k in (ZZ, YY, XX, CORE, HALO):
        @pl.when(late[k] == 0)
        def _(k=k):
            pl.semaphore_signal(barrier, inc=1, device_id=(partner[k],), device_id_type=MESH)

    pulls = [
        pltpu.make_async_copy(src, dst, local_sem.at[i])
        for i, (src, dst) in enumerate(
            ((f_hbm, own), (wq_hbm, wq), (wk_hbm, wk), (wv_hbm, wv),
             (lb_hbm, lb), (lc_hbm, lc), (eb_hbm, eb), (ec_hbm, ec))
        )
    ]
    for pull in pulls:
        pull.start()

    def copies(k):
        if k == HALO:
            src = f_hbm.at[pl.ds(pl.multiple_of(odd * BLK, BLK), BLK)]
            dst = kv.at[k, pl.ds(0, BLK)]
        else:
            src, dst = f_hbm, kv.at[k]
        return pltpu.make_async_remote_copy(
            src_ref=src, dst_ref=dst, send_sem=send_sem.at[k], recv_sem=recv_sem.at[k],
            device_id=(partner[k],), device_id_type=MESH,
        )

    moves = [copies(k) for k in range(5)]
    greeted = late[0] + late[1] + late[2] + late[3] + late[4]

    @pl.when(greeted > 0)
    def _():
        pl.semaphore_wait(barrier, greeted)

    for k in (ZZ, YY, XX, CORE, HALO):
        @pl.when(late[k] == 1)
        def _(k=k):
            pl.semaphore_signal(ready_sem.at[k], inc=1, device_id=(partner[k],), device_id_type=MESH)
            moves[k].start()

    for i in range(4):
        pulls[i].wait()
    own_rows = own[...]
    scale = LOG2E * float(head) ** (-0.5)
    qt = (dot(wq[...], own_rows, ((0,), (1,))) * scale).astype(BF16)
    wvt[...] = wv[...].T
    for h in range(HEADS):
        parts = [qt[h * head:(h + 1) * head]]
        if h:
            parts.insert(0, jnp.zeros((h * head, rows), BF16))
        if h < HEADS - 1:
            parts.append(jnp.zeros((width - (h + 1) * head, rows), BF16))
        g[h] = dot(wk[...], jnp.concatenate(parts, axis=0), ((1,), (0,))).astype(BF16)

    for k in (CORE, HALO, XX, YY, ZZ):
        @pl.when(late[k] == 0)
        def _(k=k):
            pl.semaphore_wait(ready_sem.at[k], 1)
            moves[k].start()

    for i in range(4, 8):
        pulls[i].wait()

    def put(slot, block, counts):
        row = [
            jnp.full((1, BLK), jnp.where(c == 0, OFF, jnp.where(c == 1, 0.0, 1.0)).astype(F32))
            for c in counts
        ]
        bias[slot, pl.ds(block, 1), :] = jnp.concatenate(row, axis=1)

    def in_local(q, position):
        used = jnp.int32(0)
        for j in range(4):
            used += jnp.where((lb[q, j] == position) & (j < lc[q]), 1, 0)
        return used

    def in_match(m, q, block):
        used = jnp.int32(0)
        for j in range(2):
            used += jnp.where((eb[q, j, m] == block) & (j < ec[q, m]), 1, 0)
        return used

    near = [[in_local(q, j) for j in range(4)] for q in range(2)]
    for b in range(2):
        put(0, b, [near[q][1 + b] for q in range(2)])
        extra = [jnp.where(odd == b, near[q][0] if b else near[q][3], 0) for q in range(2)]
        put(1 + CORE, b, [in_match(0, q, b) + extra[q] for q in range(2)])
        for m, k in ((1, XX), (2, YY), (3, ZZ)):
            put(1 + k, b, [in_match(m, q, b) for q in range(2)])
    put(1 + HALO, 0, [jnp.where(odd == 1, near[q][3], near[q][0]) for q in range(2)])
    put(1 + HALO, 1, [jnp.int32(0)] * 2)

    kv[HALO, pl.ds(BLK, BLK), :] = jnp.zeros((BLK, width), BF16)
    for h in range(HEADS):
        vt[h, pl.ds(head, 16), :] = jnp.ones((16, rows), BF16)
    top[...] = jnp.full(top.shape, FLOOR, F32)
    acc[...] = jnp.zeros(acc.shape, F32)

    def part(keys, slot):
        values = dot(wvt[...], keys, ((1,), (1,))).astype(BF16)
        for h in range(HEADS):
            vt[h, pl.ds(0, head), :] = values[h * head:(h + 1) * head]
        for h in range(HEADS):
            scores = dot(keys, g[h], ((1,), (0,)))
            first = bias[slot, pl.ds(0, 1), :]
            second = bias[slot, pl.ds(1, 1), :]
            old = top[h]
            new = jnp.maximum(
                old,
                jnp.maximum(
                    jnp.max(scores[:BLK], axis=0, keepdims=True) + first,
                    jnp.max(scores[BLK:], axis=0, keepdims=True) + second,
                ),
            )
            top[h] = new
            weights = jnp.concatenate(
                [
                    jnp.exp2(scores[:BLK] - (new - first)).astype(BF16),
                    jnp.exp2(scores[BLK:] - (new - second)).astype(BF16),
                ],
                axis=0,
            )
            out = dot(vt[h], weights, ((1,), (0,)))
            acc[h] = acc[h] * jnp.exp2(old - new) + out[: head + 8]

    part(own_rows, 0)

    for k in range(5):
        moves[k].wait_recv()
        part(kv[k], k + 1)

    for h in range(HEADS):
        ctx_ref[pl.ds(h * head, head), :] = (
            acc[h, pl.ds(0, head), :] / acc[h, pl.ds(head, 1), :]
        ).astype(BF16)
    for k in range(5):
        moves[k].wait_send()


def finish_kernel(ctx_ref, f_ref, w_ref, o_ref):
    mixed = dot(ctx_ref[...], w_ref[...], ((0,), (0,)))
    mean = jnp.mean(mixed * mixed, axis=-1, keepdims=True)
    o_ref[...] = (f_ref[...].astype(F32) + mixed * lax.rsqrt(mean + EPS)).astype(BF16)


def shards(features, w_query, w_key, w_value, w_out, local_blocks, local_count, expander_blocks, expander_count):
    rows, width = features.shape
    head = width // HEADS
    peers = lax.axis_size("dom")
    levels = peers.bit_length() - 1
    matches = expander_blocks.shape[0]
    swaps = [m * levels // matches for m in range(matches)]
    whole = pl.BlockSpec(memory_space=pltpu.HBM)
    inside = pl.BlockSpec(memory_space=pltpu.VMEM)
    expander_blocks = jnp.transpose(expander_blocks, (1, 2, 0))
    expander_count = expander_count.T
    ctx = pl.pallas_call(
        functools.partial(attend_kernel, peers, swaps),
        out_shape=jax.ShapeDtypeStruct((width, rows), BF16),
        in_specs=[whole] * 8,
        out_specs=inside,
        scratch_shapes=[
            pltpu.VMEM((rows, width), BF16),
            pltpu.VMEM((width, width), BF16),
            pltpu.VMEM((width, width), BF16),
            pltpu.VMEM((width, width), BF16),
            pltpu.SMEM(local_blocks.shape, jnp.int32),
            pltpu.SMEM(local_count.shape, jnp.int32),
            pltpu.SMEM(expander_blocks.shape, jnp.int32),
            pltpu.SMEM(expander_count.shape, jnp.int32),
            pltpu.VMEM((5, rows, width), BF16),
            pltpu.VMEM((HEADS, width, rows), BF16),
            pltpu.VMEM((width, width), BF16),
            pltpu.VMEM((HEADS, head + 16, rows), BF16),
            pltpu.VMEM((6, 8, rows), F32),
            pltpu.VMEM((HEADS, 1, rows), F32),
            pltpu.VMEM((HEADS, head + 8, rows), F32),
            pltpu.SemaphoreType.DMA((8,)),
            pltpu.SemaphoreType.DMA((5,)),
            pltpu.SemaphoreType.DMA((5,)),
            pltpu.SemaphoreType.REGULAR((5,)),
        ],
        compiler_params=pltpu.CompilerParams(
            collective_id=0, has_side_effects=True
        ),
        name="attend",
    )(features, w_query, w_key, w_value, local_blocks, local_count, expander_blocks, expander_count)
    return pl.pallas_call(
        finish_kernel,
        out_shape=jax.ShapeDtypeStruct((rows, width), BF16),
        in_specs=[inside] * 3,
        out_specs=inside,
        compiler_params=pltpu.CompilerParams(vmem_limit_bytes=8 << 20),
        name="finish",
    )(ctx, features, w_out)


def solution(mesh):
    in_specs = (
        P("dom", None), P(), P(), P(), P(),
        P("dom", None), P("dom"), P(None, "dom", None), P(None, "dom"),
    )
    return jax.shard_map(
        shards, mesh=mesh, in_specs=in_specs, out_specs=P("dom", None), check_vma=False
    )
```

time: 73.1 us -> 26.1 us (0.36)
  the two profiles are of different devices: /device:TPU:64 before, /device:TPU:0 now
where the time goes in v1:
time: 26.1 us; the launch traced here: 26 us
  Pallas kernels  25 us (96%)
  local copies, waits for them, and re-layouts  0.9 us (3%)
    pallas_call x1, Pallas kernels, shards(): pl.pallas_call(functools.partial(attend_kernel, peers, swaps), out_shape=...  24.1 us
    pallas_call x1, Pallas kernels, shards(): pl.pallas_call(finish_kernel, out_shape=jax.ShapeDtypeStruct((rows, width...  0.97 us
    unnamed x6, local copies, waits for them, and re-layouts  0.9 us

profile of v1, /device:TPU:0, one launch (start us, length us, event | category | flops | bytes accessed | tf_op | source)
XLA Modules:
  0.0 26.0 jit_solution(9302388193013786167)
XLA Ops:
  0.0 0.0 copy-start
  0.0 0.0 copy-start.2
  0.0 24.1 %attend.1.ctx_ref = bf16[256,256]{1,0:T(8,128)(2,1)} custom-call(bf16[256,256]{1,0:T(8,128)(2,1)} %f_ref.1, bf16[256,256]{1,0:T(8,128)(2,1)} %wq_hbm.1, bf16[256,256]{1,0:T(8,128)(2,1)} %wk_hbm.1, bf16[256,256]{1,0:T(8,128)(2,1)} %wv_hbm.1, s32[2,4]{1,0:T(2,128)} %lb_hbm.1, s32[2]{0:T(128)} %lc_hbm.1, s32[2,2,4]{2,1,0:T(2,128)} %bitcast.2, s32[2,4]{1,0:T(2,128)} %bitcast.3), custom_call_target="tpu_custom_call" | custom-call | tf_op jit(solution)/shard_map/attend/pallas_call | solution.py:217
  24.1 0.0 copy-done
  24.1 0.0 copy-done.2
  24.1 0.0 copy-start.1
  24.1 0.9 %copy-done.1 = bf16[256,256]{1,0:T(8,128)(2,1)S(1)} copy-done((bf16[256,256]{1,0:T(8,128)(2,1)S(1)}, bf16[256,256]{1,0:T(8,128)(2,1)}, u32[]{:S(2)}) %copy-start.1) | copy-done | bytes 131096
  25.0 1.0 %finish.1 = bf16[256,256]{1,0:T(8,128)(2,1)} custom-call(bf16[256,256]{1,0:T(8,128)(2,1)S(1)} %copy-done.1, bf16[256,256]{1,0:T(8,128)(2,1)S(1)} %copy-done, bf16[256,256]{1,0:T(8,128)(2,1)S(1)} %copy-done.2), custom_call_target="tpu_custom_call" | custom-call | tf_op jit(solution)/shard_map/finish/pallas_call | solution.py:248
Async XLA Ops:
  0.0 24.1 %copy-start = (bf16[256,256]{1,0:T(8,128)(2,1)S(1)}, bf16[256,256]{1,0:T(8,128)(2,1)}, u32[]{:S(2)}) copy-start(bf16[256,256]{1,0:T(8,128)(2,1)} %f_ref.1) | copy-start | bytes 393220
  0.0 24.1 %copy-start.2 = (bf16[256,256]{1,0:T(8,128)(2,1)S(1)}, bf16[256,256]{1,0:T(8,128)(2,1)}, u32[]{:S(2)}) copy-start(bf16[256,256]{1,0:T(8,128)(2,1)} %w_ref.1) | copy-start | bytes 393220
  24.1 0.9 %copy-start.1 = (bf16[256,256]{1,0:T(8,128)(2,1)S(1)}, bf16[256,256]{1,0:T(8,128)(2,1)}, u32[]{:S(2)}) copy-start(bf16[256,256]{1,0:T(8,128)(2,1)} %attend.1.ctx_ref) | copy-start | bytes 393220

commit v2 on v1

--- a/solution.py
+++ b/solution.py
@@ -33,7 +33,7 @@
     f_hbm, wq_hbm, wk_hbm, wv_hbm, lb_hbm, lc_hbm, eb_hbm, ec_hbm,
     ctx_ref,
     own, wq, wk, wv, lb, lc, eb, ec,
-    kv, g, wvt, vt, bias, top, acc,
+    kv, g, wvt, vt, bias, top, acc, raw,
     local_sem, send_sem, recv_sem, ready_sem,
 ):
     me = lax.axis_index("dom")
@@ -161,7 +161,9 @@
         for h in range(HEADS):
             vt[h, pl.ds(0, head), :] = values[h * head:(h + 1) * head]
         for h in range(HEADS):
-            scores = dot(keys, g[h], ((1,), (0,)))
+            raw[h] = dot(keys, g[h], ((1,), (0,)))
+        for h in range(HEADS):
+            scores = raw[h]
             first = bias[slot, pl.ds(0, 1), :]
             second = bias[slot, pl.ds(1, 1), :]
             old = top[h]
@@ -235,16 +237,17 @@
             pltpu.VMEM((6, 8, rows), F32),
             pltpu.VMEM((HEADS, 1, rows), F32),
             pltpu.VMEM((HEADS, head + 8, rows), F32),
+            pltpu.VMEM((HEADS, rows, rows), F32),
             pltpu.SemaphoreType.DMA((8,)),
             pltpu.SemaphoreType.DMA((5,)),
             pltpu.SemaphoreType.DMA((5,)),
             pltpu.SemaphoreType.REGULAR((5,)),
         ],
         compiler_params=pltpu.CompilerParams(
-            collective_id=0, has_side_effects=True
+            collective_id=0, has_side_effects=True, vmem_limit_bytes=32 << 20
         ),
         name="attend",
-    )(features, w_query, w_key, w_value, local_blocks, local_count, expander_blocks, expander_count)
+    )(*[pltpu.with_memory_space_constraint(a, pltpu.HBM) for a in (features, w_query, w_key, w_value, local_blocks, local_count, expander_blocks, expander_count)])
     return pl.pallas_call(
         finish_kernel,
         out_shape=jax.ShapeDtypeStruct((rows, width), BF16),

time: 26.1 us -> 16.3 us (0.62)
  the two profiles are of different devices: /device:TPU:0 before, /device:TPU:388 now
where the time goes in v2:
time: 16.3 us; the launch traced here: 16.2 us
  Pallas kernels  16.2 us (99%)
    pallas_call x1, Pallas kernels, shards(): pl.pallas_call(functools.partial(attend_kernel, peers, swaps), out_shape=...  15.2 us
    pallas_call x1, Pallas kernels, shards(): pl.pallas_call(finish_kernel, out_shape=jax.ShapeDtypeStruct((rows, width...  0.98 us

profile of v2, /device:TPU:388, one launch (start us, length us, event | category | flops | bytes accessed | tf_op | source)
XLA Modules:
  0.0 16.2 jit_solution(14500097914582291095)
XLA Ops:
  0.0 0.0 copy-start
  0.0 0.0 copy-start.1
  0.0 15.2 %attend.1.ctx_ref = bf16[256,256]{1,0:T(8,128)(2,1)S(1)} custom-call(bf16[256,256]{1,0:T(8,128)(2,1)} %f_ref.1, bf16[256,256]{1,0:T(8,128)(2,1)} %wq_hbm.1, bf16[256,256]{1,0:T(8,128)(2,1)} %wk_hbm.1, bf16[256,256]{1,0:T(8,128)(2,1)} %wv_hbm.1, s32[2,4]{1,0:T(2,128)} %lb_hbm.1, s32[2]{0:T(128)} %lc_hbm.1, s32[2,2,4]{2,1,0:T(2,128)} %bitcast.2, s32[2,4]{1,0:T(2,128)} %bitcast.3), custom_call_target="tpu_custom_call" | custom-call | tf_op jit(solution)/shard_map/attend/pallas_call | solution.py:219
  15.2 0.0 copy-done
  15.2 0.0 copy-done.1
  15.2 1.0 %finish.1 = bf16[256,256]{1,0:T(8,128)(2,1)} custom-call(bf16[256,256]{1,0:T(8,128)(2,1)S(1)} %attend.1.ctx_ref, bf16[256,256]{1,0:T(8,128)(2,1)S(1)} %copy-done, bf16[256,256]{1,0:T(8,128)(2,1)S(1)} %copy-done.1), custom_call_target="tpu_custom_call" | custom-call | tf_op jit(solution)/shard_map/finish/pallas_call | solution.py:251
Async XLA Ops:
  0.0 15.2 %copy-start = (bf16[256,256]{1,0:T(8,128)(2,1)S(1)}, bf16[256,256]{1,0:T(8,128)(2,1)}, u32[]{:S(2)}) copy-start(bf16[256,256]{1,0:T(8,128)(2,1)} %f_ref.1) | copy-start | bytes 393220
  0.0 15.2 %copy-start.1 = (bf16[256,256]{1,0:T(8,128)(2,1)S(1)}, bf16[256,256]{1,0:T(8,128)(2,1)}, u32[]{:S(2)}) copy-start(bf16[256,256]{1,0:T(8,128)(2,1)} %w_ref.1) | copy-start | bytes 393220

commit v3 on v2

--- a/solution.py
+++ b/solution.py
@@ -17,6 +17,7 @@
 F32 = jnp.float32
 BF16 = jnp.bfloat16
 CORE, XX, YY, HALO, ZZ = range(5)
+MOVES = 6
 
 
 def flip(me, apart):
@@ -34,7 +35,7 @@
     ctx_ref,
     own, wq, wk, wv, lb, lc, eb, ec,
     kv, g, wvt, vt, bias, top, acc, raw,
-    local_sem, send_sem, recv_sem, ready_sem,
+    local_sem, send_sem, recv_sem, ok_sem, ready_sem,
 ):
     me = lax.axis_index("dom")
     odd = me % 2
@@ -42,27 +43,49 @@
     width = own.shape[1]
     head = width // HEADS
     beside = lax.rem(me + 2 * odd - 1 + peers, peers)
-    partner = [flip(me, swaps[0]), flip(me, swaps[1]), flip(me, swaps[2]), beside, flip(me, swaps[3])]
-
-    def waits(apart):
-        low = 1 << apart
-        usual = (me // low) % 2
-        return jnp.where(me == 0, 1, jnp.where(me == low, 0, usual))
-
-    even_end = me + odd
-    late = [
-        1 - odd,
-        waits(swaps[1]),
-        waits(swaps[2]),
-        jnp.where(even_end % 8 == 0, odd, 1 - odd),
-        waits(swaps[3]),
-    ]
-
+    far = {XX: 1 << swaps[1], YY: 1 << swaps[2], ZZ: 1 << swaps[3]}
+    partner = {
+        CORE: flip(me, swaps[0]), XX: flip(me, swaps[1]), YY: flip(me, swaps[2]),
+        HALO: beside, ZZ: flip(me, swaps[3]),
+    }
+
+    cut = 3 * peers // 4
+    late_halo = (me == peers - 1) | (me == cut - 1)
+    even = odd == 0
+    bit = {k: (me // far[k]) % 2 for k in (XX, YY, ZZ)}
+    upper = bit[ZZ] == 1
+    plane = 2 * far[YY]
+    beyond = me >= peers // 2
+
+    def precedes(who, by):
+        return (who % plane == plane - by) & (upper | beyond)
+
+    apart = precedes(me, 1)
+    stands_in = precedes(me, 2)
+    late = {k: (me == 0) | ((bit[k] == 1) & (me != far[k])) for k in (XX, YY)}
     barrier = pltpu.get_barrier_semaphore()
-    for k in (ZZ, YY, XX, CORE, HALO):
-        @pl.when(late[k] == 0)
-        def _(k=k):
-            pl.semaphore_signal(barrier, inc=1, device_id=(partner[k],), device_id_type=MESH)
+
+    def greet(who):
+        pl.semaphore_signal(barrier, inc=1, device_id=(who,), device_id_type=MESH)
+
+    def tell(sem, who):
+        pl.semaphore_signal(sem, inc=1, device_id=(who,), device_id_type=MESH)
+
+    @pl.when(me > 0)
+    def _():
+        q = partner[ZZ]
+        greet(jnp.where(q == 1, 1, q - q % 2))
+        greet(partner[CORE])
+        for k in (YY, XX):
+            @pl.when(jnp.logical_not(late[k]))
+            def _(k=k):
+                q = partner[k]
+                r = q + 1 - q % 2
+                greet(jnp.where(q == 0, 0, jnp.where(precedes(r, 1), r - 1, r)))
+
+    @pl.when(jnp.logical_not(late_halo))
+    def _():
+        greet(jnp.where(precedes(me, 3), beside, beside + odd))
 
     pulls = [
         pltpu.make_async_copy(src, dst, local_sem.at[i])
@@ -74,29 +97,141 @@
     for pull in pulls:
         pull.start()
 
-    def copies(k):
-        if k == HALO:
-            src = f_hbm.at[pl.ds(pl.multiple_of(odd * BLK, BLK), BLK)]
-            dst = kv.at[k, pl.ds(0, BLK)]
-        else:
-            src, dst = f_hbm, kv.at[k]
+    def move(i, src, dst, who):
         return pltpu.make_async_remote_copy(
-            src_ref=src, dst_ref=dst, send_sem=send_sem.at[k], recv_sem=recv_sem.at[k],
-            device_id=(partner[k],), device_id_type=MESH,
+            src_ref=src, dst_ref=dst, send_sem=send_sem.at[i], recv_sem=recv_sem.at[i],
+            device_id=(who,), device_id_type=MESH,
         )
 
-    moves = [copies(k) for k in range(5)]
-    greeted = late[0] + late[1] + late[2] + late[3] + late[4]
-
-    @pl.when(greeted > 0)
-    def _():
-        pl.semaphore_wait(barrier, greeted)
-
-    for k in (ZZ, YY, XX, CORE, HALO):
-        @pl.when(late[k] == 1)
-        def _(k=k):
-            pl.semaphore_signal(ready_sem.at[k], inc=1, device_id=(partner[k],), device_id_type=MESH)
-            moves[k].start()
+    top_half, low_half = pl.ds(0, BLK), pl.ds(BLK, BLK)
+    shared = pl.ds(pl.multiple_of(odd * BLK, BLK), BLK)
+    moves = [move(k, f_hbm, kv.at[k], partner[k]) for k in (CORE, XX, YY)] + [
+        move(HALO, f_hbm.at[shared], kv.at[HALO, top_half], beside),
+        move(ZZ, f_hbm.at[top_half], kv.at[ZZ, top_half], partner[ZZ]),
+        move(ZZ + 1, f_hbm.at[low_half], kv.at[ZZ, low_half], partner[ZZ]),
+    ]
+
+    def send(k):
+        moves[k].start()
+        if k == ZZ:
+            moves[ZZ + 1].start()
+
+    def give_ready(mate):
+        for k in (YY, XX):
+            @pl.when(bit[k] == 1)
+            def _(k=k):
+                tell(ready_sem.at[k], partner[k])
+
+                @pl.when(partner[k] + mate != 0)
+                def _():
+                    tell(ready_sem.at[k], partner[k] + mate)
+
+    def send_late():
+        for k in (YY, XX):
+            @pl.when(late[k])
+            def _(k=k):
+                send(k)
+
+    def even_hears():
+        usual = jnp.where(stands_in, 8, 3)
+        pl.semaphore_wait(barrier, jnp.where(me == 0, 4, jnp.where(me == far[ZZ], 2, usual)))
+
+        @pl.when(me == 0)
+        def _():
+            for k in (ZZ, YY, XX, CORE):
+                tell(ready_sem.at[k], partner[k])
+            for k in (CORE, ZZ, YY, XX):
+                send(k)
+
+        @pl.when(me > 0)
+        def _():
+            tell(ok_sem, partner[CORE])
+
+            @pl.when(me != far[ZZ])
+            def _():
+                send(ZZ)
+
+            send(CORE)
+
+        @pl.when(stands_in)
+        def _():
+            give_ready(1)
+            send(HALO)
+            send_late()
+
+    def even_told():
+        pl.semaphore_wait(ok_sem, 1)
+
+        @pl.when(me != cut)
+        def _():
+            send(HALO)
+
+        send_late()
+
+    def odd_told():
+        pl.semaphore_wait(ok_sem, 1)
+        send(ZZ)
+
+        @pl.when(apart)
+        def _():
+            send_late()
+
+    def odd_hears():
+        usual = 3 + 2 * bit[XX] + 2 * bit[YY]
+        fewer = (me == far[XX] + 1) | (me == far[YY] + 1) | (me == cut + 1)
+        count = jnp.where((me == 1) | apart, 2, jnp.where(fewer, usual - 1, usual))
+        pl.semaphore_wait(barrier, count)
+
+        @pl.when(late_halo)
+        def _():
+            tell(ready_sem.at[HALO], beside)
+
+        @pl.when((me > 1) & jnp.logical_not(apart))
+        def _():
+            tell(ok_sem, partner[CORE])
+            give_ready(-1)
+
+        @pl.when(me == 1)
+        def _():
+            send(ZZ)
+
+        send(HALO)
+
+        @pl.when(me > 1)
+        def _():
+            send(CORE)
+
+        @pl.when(jnp.logical_not(apart))
+        def _():
+            send_late()
+
+    corner = me % plane <= 1
+    even_z_first = upper | beyond | corner
+    odd_z_first = (upper | corner) & (me > 1) & jnp.logical_not(apart)
+
+    @pl.when(even & even_z_first)
+    def _():
+        even_hears()
+
+    @pl.when((odd == 1) & odd_z_first)
+    def _():
+        odd_told()
+
+    @pl.when((odd == 1) & jnp.logical_not(corner))
+    def _():
+        odd_hears()
+
+    @pl.when(even & jnp.logical_not(corner | stands_in))
+    def _():
+        even_told()
+
+    @pl.when(even & jnp.logical_not(even_z_first))
+    def _():
+        even_hears()
+
+    @pl.when((odd == 1) & (beyond | apart) & jnp.logical_not(odd_z_first))
+    def _():
+        odd_told()
 
     for i in range(4):
         pulls[i].wait()
@@ -112,11 +247,23 @@
             parts.append(jnp.zeros((width - (h + 1) * head, rows), BF16))
         g[h] = dot(wk[...], jnp.concatenate(parts, axis=0), ((1,), (0,))).astype(BF16)
 
-    for k in (CORE, HALO, XX, YY, ZZ):
-        @pl.when(late[k] == 0)
+    @pl.when((odd == 1) & corner)
+    def _():
+        odd_hears()
+
+    @pl.when(even & corner & (me > 0))
+    def _():
+        even_told()
+
+    for k in (XX, YY):
+        @pl.when(jnp.logical_not(late[k]) & (me != far[k]))
         def _(k=k):
             pl.semaphore_wait(ready_sem.at[k], 1)
-            moves[k].start()
+            send(k)
+
+    @pl.when((odd == 1) & jnp.logical_not(beyond | apart | odd_z_first) & (me > 1))
+    def _():
+        odd_told()
 
     for i in range(4, 8):
         pulls[i].wait()
@@ -148,55 +295,108 @@
         for m, k in ((1, XX), (2, YY), (3, ZZ)):
             put(1 + k, b, [in_match(m, q, b) for q in range(2)])
     put(1 + HALO, 0, [jnp.where(odd == 1, near[q][3], near[q][0]) for q in range(2)])
-    put(1 + HALO, 1, [jnp.int32(0)] * 2)
-
-    kv[HALO, pl.ds(BLK, BLK), :] = jnp.zeros((BLK, width), BF16)
+
     for h in range(HEADS):
         vt[h, pl.ds(head, 16), :] = jnp.ones((16, rows), BF16)
     top[...] = jnp.full(top.shape, FLOOR, F32)
     acc[...] = jnp.zeros(acc.shape, F32)
 
-    def part(keys, slot):
+    def part(keys, slot, blocks):
+        span = BLK * len(blocks)
         values = dot(wvt[...], keys, ((1,), (1,))).astype(BF16)
         for h in range(HEADS):
-            vt[h, pl.ds(0, head), :] = values[h * head:(h + 1) * head]
+            vt[h, pl.ds(0, head), pl.ds(0, span)] = values[h * head:(h + 1) * head]
         for h in range(HEADS):
-            raw[h] = dot(keys, g[h], ((1,), (0,)))
+            raw[h, pl.ds(0, span)] = dot(keys, g[h], ((1,), (0,)))
+        offsets = [bias[slot, pl.ds(b, 1), :] for b in blocks]
         for h in range(HEADS):
-            scores = raw[h]
-            first = bias[slot, pl.ds(0, 1), :]
-            second = bias[slot, pl.ds(1, 1), :]
+            scores = [raw[h, pl.ds(i * BLK, BLK)] for i in range(len(blocks))]
             old = top[h]
-            new = jnp.maximum(
-                old,
-                jnp.maximum(
-                    jnp.max(scores[:BLK], axis=0, keepdims=True) + first,
-                    jnp.max(scores[BLK:], axis=0, keepdims=True) + second,
-                ),
-            )
+            new = old
+            for score, offset in zip(scores, offsets):
+                new = jnp.maximum(new, jnp.max(score, axis=0, keepdims=True) + offset)
             top[h] = new
-            weights = jnp.concatenate(
-                [
-                    jnp.exp2(scores[:BLK] - (new - first)).astype(BF16),
-                    jnp.exp2(scores[BLK:] - (new - second)).astype(BF16),
-                ],
-                axis=0,
-            )
-            out = dot(vt[h], weights, ((1,), (0,)))
+            weights = [
+                jnp.exp2(score - (new - offset)).astype(BF16)
+                for score, offset in zip(scores, offsets)
+            ]
+            weights = jnp.concatenate(weights, axis=0) if len(blocks) > 1 else weights[0]
+            out = dot(vt[h, :, pl.ds(0, span)], weights, ((1,), (0,)))
             acc[h] = acc[h] * jnp.exp2(old - new) + out[: head + 8]
 
-    part(own_rows, 0)
-
-    for k in range(5):
-        moves[k].wait_recv()
-        part(kv[k], k + 1)
+    part(own_rows, 0, (0, 1))
+
+    def answer(who, k):
+        @pl.when(me == who)
+        def _():
+            pl.semaphore_wait(ready_sem.at[k], 1)
+            send(k)
+
+    for who, k in ((1, CORE), (far[XX], XX), (far[YY], YY), (far[ZZ], ZZ), (cut, HALO)):
+        answer(who, k)
+
+    def full(k):
+        move(k, f_hbm, kv.at[k], partner[CORE]).wait_recv()
+        part(kv[k], k + 1, (0, 1))
+
+    def halo():
+        moves[HALO].wait_recv()
+        part(kv[HALO, top_half], 1 + HALO, (0,))
+
+    def half(b):
+        moves[ZZ + b].wait_recv()
+        part(kv[ZZ, (top_half, low_half)[b]], 1 + ZZ, (b,))
+
+    wraps = (me % plane == 0) | (me % plane == 2) | (me % plane == plane - 1)
+    inner = (me // plane) % 2 != bit[ZZ]
+
+    @pl.when(me != 1)
+    def _():
+        full(CORE)
+
+    @pl.when(jnp.logical_not(wraps))
+    def _():
+        halo()
+
+    @pl.when(inner)
+    def _():
+        half(0)
+        half(1)
+
+    @pl.when(jnp.logical_not(corner))
+    def _():
+        full(YY)
+
+    @pl.when(jnp.logical_not(inner))
+    def _():
+        half(0)
+
+    full(XX)
+
+    @pl.when(jnp.logical_not(inner))
+    def _():
+        half(1)
+
+    @pl.when(corner)
+    def _():
+        full(YY)
+
+    @pl.when(me == 1)
+    def _():
+        full(CORE)
+
+    answer(0, HALO)
+
+    @pl.when(wraps)
+    def _():
+        halo()
 
     for h in range(HEADS):
         ctx_ref[pl.ds(h * head, head), :] = (
             acc[h, pl.ds(0, head), :] / acc[h, pl.ds(head, 1), :]
         ).astype(BF16)
-    for k in range(5):
-        moves[k].wait_send()
+    for i in range(MOVES):
+        moves[i].wait_send()
 
 
 def finish_kernel(ctx_ref, f_ref, w_ref, o_ref):
@@ -239,8 +439,9 @@
             pltpu.VMEM((HEADS, head + 8, rows), F32),
             pltpu.VMEM((HEADS, rows, rows), F32),
             pltpu.SemaphoreType.DMA((8,)),
-            pltpu.SemaphoreType.DMA((5,)),
-            pltpu.SemaphoreType.DMA((5,)),
+            pltpu.SemaphoreType.DMA((MOVES,)),
+            pltpu.SemaphoreType.DMA((MOVES,)),
+            pltpu.SemaphoreType.REGULAR,
             pltpu.SemaphoreType.REGULAR((5,)),
         ],
         compiler_params=pltpu.CompilerParams(

time: 16.3 us -> 15.4 us (0.945)
  the two profiles are of different devices: /device:TPU:388 before, /device:TPU:31 now
where the time goes in v3:
time: 15.4 us; the launch traced here: 15.3 us
  Pallas kernels  15.2 us (99%)
    pallas_call x1, Pallas kernels, shards(): pl.pallas_call(functools.partial(attend_kernel, peers, swaps), out_shape=...  14.3 us
    pallas_call x1, Pallas kernels, shards(): pl.pallas_call(finish_kernel, out_shape=jax.ShapeDtypeStruct((rows, width...  0.98 us

profile of v3, /device:TPU:31, one launch (start us, length us, event | category | flops | bytes accessed | tf_op | source)
XLA Modules:
  0.0 15.3 jit_solution(967530404241154183)
XLA Ops:
  0.0 0.0 copy-start
  0.0 0.0 copy-start.1
  0.0 14.3 %attend.1.ctx_ref = bf16[256,256]{1,0:T(8,128)(2,1)S(1)} custom-call(bf16[256,256]{1,0:T(8,128)(2,1)} %f_ref.1, bf16[256,256]{1,0:T(8,128)(2,1)} %wq_hbm.1, bf16[256,256]{1,0:T(8,128)(2,1)} %wk_hbm.1, bf16[256,256]{1,0:T(8,128)(2,1)} %wv_hbm.1, s32[2,4]{1,0:T(2,128)} %lb_hbm.1, s32[2]{0:T(128)} %lc_hbm.1, s32[2,2,4]{2,1,0:T(2,128)} %bitcast.2, s32[2,4]{1,0:T(2,128)} %bitcast.3), custom_call_target="tpu_custom_call" | custom-call | tf_op jit(solution)/shard_map/attend/pallas_call | solution.py:419
  14.3 0.0 copy-done
  14.3 0.0 copy-done.1
  14.3 1.0 %finish.1 = bf16[256,256]{1,0:T(8,128)(2,1)} custom-call(bf16[256,256]{1,0:T(8,128)(2,1)S(1)} %attend.1.ctx_ref, bf16[256,256]{1,0:T(8,128)(2,1)S(1)} %copy-done, bf16[256,256]{1,0:T(8,128)(2,1)S(1)} %copy-done.1), custom_call_target="tpu_custom_call" | custom-call | tf_op jit(solution)/shard_map/finish/pallas_call | solution.py:452
Async XLA Ops:
  0.0 14.3 %copy-start = (bf16[256,256]{1,0:T(8,128)(2,1)S(1)}, bf16[256,256]{1,0:T(8,128)(2,1)}, u32[]{:S(2)}) copy-start(bf16[256,256]{1,0:T(8,128)(2,1)} %f_ref.1) | copy-start | bytes 393220
  0.0 14.3 %copy-start.1 = (bf16[256,256]{1,0:T(8,128)(2,1)S(1)}, bf16[256,256]{1,0:T(8,128)(2,1)}, u32[]{:S(2)}) copy-start(bf16[256,256]{1,0:T(8,128)(2,1)} %w_ref.1) | copy-start | bytes 393220

commit v4 on v3

--- a/solution.py
+++ b/solution.py
@@ -58,7 +58,7 @@
     beyond = me >= peers // 2
 
     def precedes(who, by):
-        return (who % plane == plane - by) & (upper | beyond)
+        return (who % plane == plane - by) & ((upper & ((me // plane) % 2 == 1)) | beyond)
 
     apart = precedes(me, 1)
     stands_in = precedes(me, 2)
@@ -363,18 +363,24 @@
         half(0)
         half(1)
 
+    edge = me % (2 * far[XX]) <= 1
+
+    @pl.when(edge & jnp.logical_not(inner))
+    def _():
+        half(0)
+
     @pl.when(jnp.logical_not(corner))
     def _():
         full(YY)
 
+    @pl.when(jnp.logical_not(edge | inner))
+    def _():
+        half(0)
+
+    full(XX)
+
     @pl.when(jnp.logical_not(inner))
     def _():
-        half(0)
-
-    full(XX)
-
-    @pl.when(jnp.logical_not(inner))
-    def _():
         half(1)
 
     @pl.when(corner)
@@ -392,17 +398,24 @@
         halo()
 
     for h in range(HEADS):
-        ctx_ref[pl.ds(h * head, head), :] = (
-            acc[h, pl.ds(0, head), :] / acc[h, pl.ds(head, 1), :]
-        ).astype(BF16)
+        share = 1.0 / acc[h, pl.ds(head, 1), :]
+        ctx_ref[pl.ds(h * head, head), :] = (acc[h, pl.ds(0, head), :] * share).astype(BF16)
     for i in range(MOVES):
         moves[i].wait_send()
 
 
-def finish_kernel(ctx_ref, f_ref, w_ref, o_ref):
-    mixed = dot(ctx_ref[...], w_ref[...], ((0,), (0,)))
-    mean = jnp.mean(mixed * mixed, axis=-1, keepdims=True)
-    o_ref[...] = (f_ref[...].astype(F32) + mixed * lax.rsqrt(mean + EPS)).astype(BF16)
+def finish_kernel(ctx_ref, f_ref, w_ref, o_hbm, done, sem):
+    rows = f_ref.shape[0]
+    copies = []
+    for b in range(rows // BLK):
+        block = pl.ds(b * BLK, BLK)
+        mixed = dot(ctx_ref[:, block], w_ref[...], ((0,), (0,)))
+        mean = jnp.mean(mixed * mixed, axis=-1, keepdims=True)
+        done[block, :] = (f_ref[block, :].astype(F32) + mixed * lax.rsqrt(mean + EPS)).astype(BF16)
+        copies.append(pltpu.make_async_copy(done.at[block], o_hbm.at[block], sem.at[b]))
+        copies[-1].start()
+    for copy in copies:
+        copy.wait()
 
 
 def shards(features, w_query, w_key, w_value, w_out, local_blocks, local_count, expander_blocks, expander_count):
@@ -453,7 +466,8 @@
         finish_kernel,
         out_shape=jax.ShapeDtypeStruct((rows, width), BF16),
         in_specs=[inside] * 3,
-        out_specs=inside,
+        out_specs=whole,
+        scratch_shapes=[pltpu.VMEM((rows, width), BF16), pltpu.SemaphoreType.DMA((rows // BLK,))],
         compiler_params=pltpu.CompilerParams(vmem_limit_bytes=8 << 20),
         name="finish",
     )(ctx, features, w_out)

time: 15.4 us -> 14.8 us (0.961)
  the two profiles are of different devices: /device:TPU:31 before, /device:TPU:128 now
where the time goes in v4:
time: 14.8 us; the launch traced here: 14.6 us
  Pallas kernels  14.6 us (99%)
    pallas_call x1, Pallas kernels, shards(): pl.pallas_call(functools.partial(attend_kernel, peers, swaps), out_shape=...  13.6 us
    pallas_call x1, Pallas kernels, shards(): pl.pallas_call(finish_kernel, out_shape=jax.ShapeDtypeStruct((rows, width...  0.98 us

profile of v4, /device:TPU:128, one launch (start us, length us, event | category | flops | bytes accessed | tf_op | source)
XLA Modules:
  0.0 14.6 jit_solution(9475729839236992662)
XLA Ops:
  0.0 0.0 copy-start
  0.0 0.0 copy-start.1
  0.0 13.6 %attend.1.ctx_ref = bf16[256,256]{1,0:T(8,128)(2,1)S(1)} custom-call(bf16[256,256]{1,0:T(8,128)(2,1)} %f_ref.1, bf16[256,256]{1,0:T(8,128)(2,1)} %wq_hbm.1, bf16[256,256]{1,0:T(8,128)(2,1)} %wk_hbm.1, bf16[256,256]{1,0:T(8,128)(2,1)} %wv_hbm.1, s32[2,4]{1,0:T(2,128)} %lb_hbm.1, s32[2]{0:T(128)} %lc_hbm.1, s32[2,2,4]{2,1,0:T(2,128)} %bitcast.2, s32[2,4]{1,0:T(2,128)} %bitcast.3), custom_call_target="tpu_custom_call" | custom-call | tf_op jit(solution)/shard_map/attend/pallas_call | solution.py:432
  13.6 0.0 copy-done
  13.7 0.0 copy-done.1
  13.7 1.0 %finish.1 = bf16[256,256]{1,0:T(8,128)(2,1)} custom-call(bf16[256,256]{1,0:T(8,128)(2,1)S(1)} %attend.1.ctx_ref, bf16[256,256]{1,0:T(8,128)(2,1)S(1)} %copy-done, bf16[256,256]{1,0:T(8,128)(2,1)S(1)} %copy-done.1), custom_call_target="tpu_custom_call" | custom-call | tf_op jit(solution)/shard_map/finish/pallas_call | solution.py:465
Async XLA Ops:
  0.0 13.6 %copy-start = (bf16[256,256]{1,0:T(8,128)(2,1)S(1)}, bf16[256,256]{1,0:T(8,128)(2,1)}, u32[]{:S(2)}) copy-start(bf16[256,256]{1,0:T(8,128)(2,1)} %f_ref.1) | copy-start | bytes 393220
  0.0 13.7 %copy-start.1 = (bf16[256,256]{1,0:T(8,128)(2,1)S(1)}, bf16[256,256]{1,0:T(8,128)(2,1)}, u32[]{:S(2)}) copy-start(bf16[256,256]{1,0:T(8,128)(2,1)} %w_ref.1) | copy-start | bytes 393220

commit v5 on v4

--- a/solution.py
+++ b/solution.py
@@ -20,9 +20,17 @@
 MOVES = 6
 
 
+def rem(a, b):
+    return lax.rem(a, jnp.int32(b))
+
+
+def div(a, b):
+    return lax.div(a, jnp.int32(b))
+
+
 def flip(me, apart):
     wide = 1 << apart
-    return me + wide - 2 * wide * ((me // wide) % 2)
+    return me + wide - 2 * wide * rem(div(me, wide), 2)
 
 
 def dot(a, b, over):
@@ -38,7 +46,7 @@
     local_sem, send_sem, recv_sem, ok_sem, ready_sem,
 ):
     me = lax.axis_index("dom")
-    odd = me % 2
+    odd = rem(me, 2)
     rows = own.shape[0]
     width = own.shape[1]
     head = width // HEADS
@@ -50,15 +58,19 @@
     }
 
     cut = 3 * peers // 4
-    late_halo = (me == peers - 1) | (me == cut - 1)
     even = odd == 0
-    bit = {k: (me // far[k]) % 2 for k in (XX, YY, ZZ)}
+    bit = {k: rem(div(me, far[k]), 2) for k in (XX, YY, ZZ)}
     upper = bit[ZZ] == 1
-    plane = 2 * far[YY]
+    row, plane = 2 * far[XX], 2 * far[YY]
+
+    def begins(who):
+        return ((rem(who, row) == 0) & (rem(who, plane) > 0)) | (who == cut)
+
+    late_halo = (odd == 1) & ((beside == 0) | begins(beside))
     beyond = me >= peers // 2
 
     def precedes(who, by):
-        return (who % plane == plane - by) & ((upper & ((me // plane) % 2 == 1)) | beyond)
+        return (rem(who, plane) == plane - by) & ((upper & (rem(div(me, plane), 2) == 1)) | beyond)
 
     apart = precedes(me, 1)
     stands_in = precedes(me, 2)
@@ -74,13 +86,13 @@
     @pl.when(me > 0)
     def _():
         q = partner[ZZ]
-        greet(jnp.where(q == 1, 1, q - q % 2))
+        greet(jnp.where(q == 1, 1, q - odd))
         greet(partner[CORE])
         for k in (YY, XX):
             @pl.when(jnp.logical_not(late[k]))
             def _(k=k):
                 q = partner[k]
-                r = q + 1 - q % 2
+                r = q + 1 - odd
                 greet(jnp.where(q == 0, 0, jnp.where(precedes(r, 1), r - 1, r)))
 
     @pl.when(jnp.logical_not(late_halo))
@@ -162,7 +174,7 @@
     def even_told():
         pl.semaphore_wait(ok_sem, 1)
 
-        @pl.when(me != cut)
+        @pl.when(jnp.logical_not(begins(me)))
         def _():
             send(HALO)
 
@@ -178,8 +190,9 @@
 
     def odd_hears():
         usual = 3 + 2 * bit[XX] + 2 * bit[YY]
-        fewer = (me == far[XX] + 1) | (me == far[YY] + 1) | (me == cut + 1)
-        count = jnp.where((me == 1) | apart, 2, jnp.where(fewer, usual - 1, usual))
+        usual -= jnp.where((me == far[XX] + 1) | (me == far[YY] + 1), 1, 0)
+        usual -= jnp.where(begins(me - 1), 1, 0)
+        count = jnp.where((me == 1) | apart, 2, usual)
         pl.semaphore_wait(barrier, count)
 
         @pl.when(late_halo)
@@ -205,7 +218,7 @@
         def _():
             send_late()
 
-    corner = me % plane <= 1
+    corner = rem(me, plane) <= 1
     even_z_first = upper | beyond | corner
     odd_z_first = (upper | corner) & (me > 1) & jnp.logical_not(apart)
 
@@ -264,6 +277,11 @@
     @pl.when((odd == 1) & jnp.logical_not(beyond | apart | odd_z_first) & (me > 1))
     def _():
         odd_told()
+
+    @pl.when(begins(me) & (me != cut))
+    def _():
+        pl.semaphore_wait(ready_sem.at[HALO], 1)
+        send(HALO)
 
     for i in range(4, 8):
         pulls[i].wait()
@@ -347,8 +365,8 @@
         moves[ZZ + b].wait_recv()
         part(kv[ZZ, (top_half, low_half)[b]], 1 + ZZ, (b,))
 
-    wraps = (me % plane == 0) | (me % plane == 2) | (me % plane == plane - 1)
-    inner = (me // plane) % 2 != bit[ZZ]
+    wraps = (rem(me, plane) == 0) | (rem(me, row) == row - 1)
+    inner = rem(div(me, plane), 2) != bit[ZZ]
 
     @pl.when(me != 1)
     def _():
@@ -363,7 +381,7 @@
         half(0)
         half(1)
 
-    edge = me % (2 * far[XX]) <= 1
+    edge = rem(me, row) <= 1
 
     @pl.when(edge & jnp.logical_not(inner))
     def _():

time: 14.8 us -> 14.7 us (level)
  no operation moved by 1% of the time
where the time goes in v5:
time: 14.7 us; the launch traced here: 14.6 us
  Pallas kernels  14.6 us (99%)
    pallas_call x1, Pallas kernels, shards(): pl.pallas_call(functools.partial(attend_kernel, peers, swaps), out_shape=...  13.6 us
    pallas_call x1, Pallas kernels, shards(): pl.pallas_call(finish_kernel, out_shape=jax.ShapeDtypeStruct((rows, width...  0.98 us

profile of v5, /device:TPU:128, one launch (start us, length us, event | category | flops | bytes accessed | tf_op | source)
XLA Modules:
  0.0 14.6 jit_solution(2442857814424786261)
XLA Ops:
  0.0 0.0 copy-start
  0.0 0.0 copy-start.1
  0.0 13.6 %attend.1.ctx_ref = bf16[256,256]{1,0:T(8,128)(2,1)S(1)} custom-call(bf16[256,256]{1,0:T(8,128)(2,1)} %f_ref.1, bf16[256,256]{1,0:T(8,128)(2,1)} %wq_hbm.1, bf16[256,256]{1,0:T(8,128)(2,1)} %wk_hbm.1, bf16[256,256]{1,0:T(8,128)(2,1)} %wv_hbm.1, s32[2,4]{1,0:T(2,128)} %lb_hbm.1, s32[2]{0:T(128)} %lc_hbm.1, s32[2,2,4]{2,1,0:T(2,128)} %bitcast.2, s32[2,4]{1,0:T(2,128)} %bitcast.3), custom_call_target="tpu_custom_call" | custom-call | tf_op jit(solution)/shard_map/attend/pallas_call | solution.py:450
  13.6 0.0 copy-done
  13.6 0.0 copy-done.1
  13.6 1.0 %finish.1 = bf16[256,256]{1,0:T(8,128)(2,1)} custom-call(bf16[256,256]{1,0:T(8,128)(2,1)S(1)} %attend.1.ctx_ref, bf16[256,256]{1,0:T(8,128)(2,1)S(1)} %copy-done, bf16[256,256]{1,0:T(8,128)(2,1)S(1)} %copy-done.1), custom_call_target="tpu_custom_call" | custom-call | tf_op jit(solution)/shard_map/finish/pallas_call | solution.py:483
Async XLA Ops:
  0.0 13.6 %copy-start = (bf16[256,256]{1,0:T(8,128)(2,1)S(1)}, bf16[256,256]{1,0:T(8,128)(2,1)}, u32[]{:S(2)}) copy-start(bf16[256,256]{1,0:T(8,128)(2,1)} %f_ref.1) | copy-start | bytes 393220
  0.0 13.6 %copy-start.1 = (bf16[256,256]{1,0:T(8,128)(2,1)S(1)}, bf16[256,256]{1,0:T(8,128)(2,1)}, u32[]{:S(2)}) copy-start(bf16[256,256]{1,0:T(8,128)(2,1)} %w_ref.1) | copy-start | bytes 393220

commit v6 on v5

--- a/solution.py
+++ b/solution.py
@@ -381,7 +381,7 @@
         half(0)
         half(1)
 
-    edge = rem(me, row) <= 1
+    edge = (rem(me, row) <= 1) | (odd == 1) | upper
 
     @pl.when(edge & jnp.logical_not(inner))
     def _():

time: 14.7 us -> 14.7 us (level)
  no operation moved by 1% of the time
where the time goes in v6:
time: 14.7 us; the launch traced here: 14.6 us
  Pallas kernels  14.6 us (99%)
    pallas_call x1, Pallas kernels, shards(): pl.pallas_call(functools.partial(attend_kernel, peers, swaps), out_shape=...  13.6 us
    pallas_call x1, Pallas kernels, shards(): pl.pallas_call(finish_kernel, out_shape=jax.ShapeDtypeStruct((rows, width...  0.98 us

profile of v6, /device:TPU:128, one launch (start us, length us, event | category | flops | bytes accessed | tf_op | source)
XLA Modules:
  0.0 14.6 jit_solution(7699277888274216424)
XLA Ops:
  0.0 0.0 copy-start
  0.0 0.0 copy-start.1
  0.0 13.6 %attend.1.ctx_ref = bf16[256,256]{1,0:T(8,128)(2,1)S(1)} custom-call(bf16[256,256]{1,0:T(8,128)(2,1)} %f_ref.1, bf16[256,256]{1,0:T(8,128)(2,1)} %wq_hbm.1, bf16[256,256]{1,0:T(8,128)(2,1)} %wk_hbm.1, bf16[256,256]{1,0:T(8,128)(2,1)} %wv_hbm.1, s32[2,4]{1,0:T(2,128)} %lb_hbm.1, s32[2]{0:T(128)} %lc_hbm.1, s32[2,2,4]{2,1,0:T(2,128)} %bitcast.2, s32[2,4]{1,0:T(2,128)} %bitcast.3), custom_call_target="tpu_custom_call" | custom-call | tf_op jit(solution)/shard_map/attend/pallas_call | solution.py:450
  13.6 0.0 copy-done
  13.6 0.0 copy-done.1
  13.6 1.0 %finish.1 = bf16[256,256]{1,0:T(8,128)(2,1)} custom-call(bf16[256,256]{1,0:T(8,128)(2,1)S(1)} %attend.1.ctx_ref, bf16[256,256]{1,0:T(8,128)(2,1)S(1)} %copy-done, bf16[256,256]{1,0:T(8,128)(2,1)S(1)} %copy-done.1), custom_call_target="tpu_custom_call" | custom-call | tf_op jit(solution)/shard_map/finish/pallas_call | solution.py:483
Async XLA Ops:
  0.0 13.6 %copy-start = (bf16[256,256]{1,0:T(8,128)(2,1)S(1)}, bf16[256,256]{1,0:T(8,128)(2,1)}, u32[]{:S(2)}) copy-start(bf16[256,256]{1,0:T(8,128)(2,1)} %f_ref.1) | copy-start | bytes 393220
  0.0 13.6 %copy-start.1 = (bf16[256,256]{1,0:T(8,128)(2,1)S(1)}, bf16[256,256]{1,0:T(8,128)(2,1)}, u32[]{:S(2)}) copy-start(bf16[256,256]{1,0:T(8,128)(2,1)} %w_ref.1) | copy-start | bytes 393220

commit v7 on v6

--- a/solution.py
+++ b/solution.py
@@ -174,11 +174,11 @@
     def even_told():
         pl.semaphore_wait(ok_sem, 1)
 
+        send_late()
+
         @pl.when(jnp.logical_not(begins(me)))
         def _():
             send(HALO)
-
-        send_late()
 
     def odd_told():
         pl.semaphore_wait(ok_sem, 1)
@@ -210,13 +210,13 @@
 
         send(HALO)
 
+        @pl.when(jnp.logical_not(apart))
+        def _():
+            send_late()
+
         @pl.when(me > 1)
         def _():
             send(CORE)
-
-        @pl.when(jnp.logical_not(apart))
-        def _():
-            send_late()
 
     corner = rem(me, plane) <= 1
     even_z_first = upper | beyond | corner

time: 14.7 us -> 14.7 us (level)
  no operation moved by 1% of the time
where the time goes in v7:
time: 14.7 us; the launch traced here: 14.6 us
  Pallas kernels  14.6 us (99%)
    pallas_call x1, Pallas kernels, shards(): pl.pallas_call(functools.partial(attend_kernel, peers, swaps), out_shape=...  13.6 us
    pallas_call x1, Pallas kernels, shards(): pl.pallas_call(finish_kernel, out_shape=jax.ShapeDtypeStruct((rows, width...  0.98 us

profile of v7, /device:TPU:128, one launch (start us, length us, event | category | flops | bytes accessed | tf_op | source)
XLA Modules:
  0.0 14.6 jit_solution(3733539062089936287)
XLA Ops:
  0.0 0.0 copy-start
  0.0 0.0 copy-start.1
  0.0 13.6 %attend.1.ctx_ref = bf16[256,256]{1,0:T(8,128)(2,1)S(1)} custom-call(bf16[256,256]{1,0:T(8,128)(2,1)} %f_ref.1, bf16[256,256]{1,0:T(8,128)(2,1)} %wq_hbm.1, bf16[256,256]{1,0:T(8,128)(2,1)} %wk_hbm.1, bf16[256,256]{1,0:T(8,128)(2,1)} %wv_hbm.1, s32[2,4]{1,0:T(2,128)} %lb_hbm.1, s32[2]{0:T(128)} %lc_hbm.1, s32[2,2,4]{2,1,0:T(2,128)} %bitcast.2, s32[2,4]{1,0:T(2,128)} %bitcast.3), custom_call_target="tpu_custom_call" | custom-call | tf_op jit(solution)/shard_map/attend/pallas_call | solution.py:450
  13.6 0.0 copy-done
  13.6 0.0 copy-done.1
  13.6 1.0 %finish.1 = bf16[256,256]{1,0:T(8,128)(2,1)} custom-call(bf16[256,256]{1,0:T(8,128)(2,1)S(1)} %attend.1.ctx_ref, bf16[256,256]{1,0:T(8,128)(2,1)S(1)} %copy-done, bf16[256,256]{1,0:T(8,128)(2,1)S(1)} %copy-done.1), custom_call_target="tpu_custom_call" | custom-call | tf_op jit(solution)/shard_map/finish/pallas_call | solution.py:483
Async XLA Ops:
  0.0 13.6 %copy-start = (bf16[256,256]{1,0:T(8,128)(2,1)S(1)}, bf16[256,256]{1,0:T(8,128)(2,1)}, u32[]{:S(2)}) copy-start(bf16[256,256]{1,0:T(8,128)(2,1)} %f_ref.1) | copy-start | bytes 393220
  0.0 13.6 %copy-start.1 = (bf16[256,256]{1,0:T(8,128)(2,1)S(1)}, bf16[256,256]{1,0:T(8,128)(2,1)}, u32[]{:S(2)}) copy-start(bf16[256,256]{1,0:T(8,128)(2,1)} %w_ref.1) | copy-start | bytes 393220
